TPU v7x, 32 devices: a whole 2x2x4 slice. The times are simulated.
32 devices in a mesh: group: 2 (over y), rows: 4 (over z), sec: 2 (over x), sub: 2 (over core).
Axes of the slice: x: 2, y: 2, z: 4, core: 2. Of those that a mesh axis runs over, the one named last changes fastest.
Arguments:
- row_seeds: int32 [16384], P(('group', 'rows')), parts along dimension 0, may hold values from 0 to 65520
- labels: int32 [16384], P(('group', 'rows')), parts along dimension 0, may hold values from 0 to 1
- weights: float32 [131072], P(('group', 'sec', 'sub')), parts along dimension 0, may hold values from -5 to 5
- sketch: bfloat16 [65536, 64], P(('sec', 'sub')), may hold values from -5 to 5
Outputs:
- step: float32 [131072], P(('group', 'sec', 'sub')), parts along dimension 0
- sketched: float32 [131072, 64], P(('group', 'sec', 'sub')), parts along dimension 0
There are 2 independent parts, one for each index of `group`. A program takes and returns all parts, laid end to end along the dimension named above; an argument that names none is the same for every part. Nothing has to cross between parts.
All inputs are finite; a program needn't handle non-finite values.
Results may differ from a plain program's by a relative error of at most 0.0029.
Values may be sent and summed in bfloat16 or wider, within the bound.
No kernel may reach another device: no remote copies, remote signals or barrier semaphores. Data moves between devices by JAX's collectives and lax.ppermute only.
A program may use at most 128 MiB of HBM per device.

v0:
```python
import jax
import jax.numpy as jnp
from jax import lax
from jax.sharding import PartitionSpec as P

ROOT = 256


def table_block(seeds, first, count):
    cols = first + lax.iota(jnp.int32, count)
    part_a = cols * 30011 % 65521
    part_b = seeds * 16411 % 65521
    mixer = (part_b[:, None] + part_a[None, :]) % 65521
    folded = mixer % 46337
    mixer = folded * folded % 65521
    mixer = (mixer * 31 + part_a[None, :] + 7) % 65521
    level = mixer % 16
    return ((level.astype(jnp.float32) - 7.5) * (1.0 / (4.0 * ROOT))).astype(jnp.bfloat16)


def block_size():
    return 512


def margin_rows(seeds, first, stacked):
    count = seeds.shape[0]
    blk = block_size()
    nblk = count // blk
    nfeat = stacked.shape[0]

    def one_block(block_seeds):
        return jnp.dot(
            table_block(block_seeds, first, nfeat), stacked, preferred_element_type=jnp.float32
        )

    return lax.map(one_block, seeds.reshape(nblk, blk)).reshape(count, stacked.shape[1])


def accumulate(seeds, mixed, first, nfeat):
    count = seeds.shape[0]
    blk = block_size()
    nblk = count // blk

    def add_block(index, acc):
        block_seeds = lax.dynamic_slice_in_dim(seeds, index * blk, blk, 0)
        block_mixed = lax.dynamic_slice_in_dim(mixed, index * blk, blk, 0)
        tab = table_block(block_seeds, first, nfeat)
        return acc + lax.dot_general(
            tab, block_mixed, (((0,), (0,)), ((), ())), preferred_element_type=jnp.float32
        )

    return lax.fori_loop(0, nblk, add_block, jnp.zeros((nfeat, mixed.shape[1]), jnp.float32))


def weigh(margins, labels):
    prob = jax.nn.sigmoid(margins[:, 0])
    resid = prob - labels.astype(jnp.float32)
    curv = prob * (1.0 - prob)
    return jnp.concatenate([resid[:, None], curv[:, None] * margins[:, 1:]], axis=1).astype(
        jnp.bfloat16
    )


def products(sketch_part, sketched, grad):
    highest = lax.Precision.HIGHEST
    core = lax.dot_general(
        sketch_part.astype(jnp.float32), sketched, (((0,), (0,)), ((), ())), precision=highest
    )
    square = lax.dot_general(sketched, sketched, (((0,), (0,)), ((), ())), precision=highest)
    proj = lax.dot_general(sketched, grad, (((0,), (0,)), ((), ())), precision=highest)
    return (core, square, proj)


def finish(core, square, proj, sketched, grad, lam):
    inner = lam * core + square
    inner = 0.5 * (inner + inner.T)
    factor = jnp.linalg.cholesky(inner)
    middle = lax.linalg.triangular_solve(factor, proj[:, None], left_side=True, lower=True)
    coef = lax.linalg.triangular_solve(
        factor, middle, left_side=True, lower=True, transpose_a=True
    )[:, 0]
    return (grad - jnp.dot(sketched, coef, precision=lax.Precision.HIGHEST)) / lam


def local(row_seeds, labels, weights, sketch):
    lam = 0.05
    nfeat = weights.shape[0]
    first = lax.axis_index(("sec", "sub")) * nfeat
    stacked = jnp.concatenate([weights.astype(jnp.bfloat16)[:, None], sketch], axis=1)
    local_margins = margin_rows(row_seeds, first, stacked)
    margins = lax.psum(local_margins, ("sec", "sub"))
    mixed = weigh(margins, labels)
    partial_total = accumulate(row_seeds, mixed, first, nfeat)
    piece = lax.psum_scatter(partial_total, "rows", scatter_dimension=0, tiled=True)
    count = piece.shape[0]
    position = lax.axis_index("rows") * count
    own_weights = lax.dynamic_slice_in_dim(weights, position, count, 0)
    own_sketch = lax.dynamic_slice_in_dim(sketch, position, count, 0)
    grad = piece[:, 0] + lam * own_weights
    sketched = piece[:, 1:] + lam * own_sketch.astype(jnp.float32)
    core, square, proj = products(own_sketch, sketched, grad)
    core, square, proj = lax.psum((core, square, proj), ("rows", "sec", "sub"))
    step = finish(core, square, proj, sketched, grad, lam)
    step, sketched = (
        lax.all_gather(step, "rows", axis=0, tiled=True),
        lax.all_gather(sketched, "rows", axis=0, tiled=True),
    )
    return (step, sketched)


def solution(mesh):
    placed = (
        P(("group", "rows")),
        P(("group", "rows")),
        P(("group", "sec", "sub")),
        P(("sec", "sub"), None),
    )
    return jax.shard_map(
        local,
        mesh=mesh,
        in_specs=placed,
        out_specs=(P(("group", "sec", "sub")), P(("group", "sec", "sub"), None)),
        check_vma=False,
    )
```

profile of v0, /device:TPU:0, one launch (start us, length us, event | category | flops | bytes accessed | tf_op | source)
XLA Modules:
  0.0 1060.1 jit_solution(18047026899343946793)
XLA Ops:
  8.1 3.8 broadcast_in_dim.39
  11.9 4.7 copy.29
  17.4 5.9 pad_maximum_fusion
  23.3 415.5 %while.30 = (s32[]{:T(128)}, f32[4,512,65]{1,0,2:T(4,128)S(1)}, s32[4,512]{1,0:T(4,128)S(1)}, s32[]{:T(128)}, bf16[16384,65]{1,0:T(8,128)(2,1)}, /*index=5*/s32[]{:T(128)}, s32[]{:T(128)}) while((s32[]{:T(128)}, f32[4,512,65]{1,0,2:T(4,128)S(1)}, s32[4,512]{1,0:T(4,128)S(1)}, s32[]{:T(128)}, bf16[16384,65]{1,0:T(8,128)(2,1)}, ...), condition=%wide.region_1.2_spmd, body=%wide.region_0.1_spmd.sunk | while | flops 1459752448 | bytes 45011060 | solution.py:36
  23.4 91.7 %fusion.121 = bf16[512,16384]{1,0:T(8,128)(2,1)} fusion(s32[16384]{0:T(1024)S(1)} %add_select_fusion.18, s32[512]{0:T(512)S(1)} %add_select_fusion.19), kind=kLoop, calls=%fused_computation.18.clone.clone.clone.clone.1.clone.1 | loop fusion | flops 369098752 | bytes 16844800 | tf_op jit(solution)/shard_map/while/body/eval_jaxpr/dot_general | solution.py:32
  115.0 8.8 fusion.122
  127.3 91.7 %fusion.121 = bf16[512,16384]{1,0:T(8,128)(2,1)} fusion(s32[16384]{0:T(1024)S(1)} %add_select_fusion.18, s32[512]{0:T(512)S(1)} %add_select_fusion.19), kind=kLoop, calls=%fused_computation.18.clone.clone.clone.clone.1.clone.1 | loop fusion | flops 369098752 | bytes 16844800 | tf_op jit(solution)/shard_map/while/body/eval_jaxpr/dot_general | solution.py:32
  218.9 8.8 fusion.122
  231.1 91.7 %fusion.121 = bf16[512,16384]{1,0:T(8,128)(2,1)} fusion(s32[16384]{0:T(1024)S(1)} %add_select_fusion.18, s32[512]{0:T(512)S(1)} %add_select_fusion.19), kind=kLoop, calls=%fused_computation.18.clone.clone.clone.clone.1.clone.1 | loop fusion | flops 369098752 | bytes 16844800 | tf_op jit(solution)/shard_map/while/body/eval_jaxpr/dot_general | solution.py:32
  322.8 8.8 fusion.122
  335.0 91.7 %fusion.121 = bf16[512,16384]{1,0:T(8,128)(2,1)} fusion(s32[16384]{0:T(1024)S(1)} %add_select_fusion.18, s32[512]{0:T(512)S(1)} %add_select_fusion.19), kind=kLoop, calls=%fused_computation.18.clone.clone.clone.clone.1.clone.1 | loop fusion | flops 369098752 | bytes 16844800 | tf_op jit(solution)/shard_map/while/body/eval_jaxpr/dot_general | solution.py:32
  426.7 8.8 fusion.122
  440.0 36.3 %all-reduce.3.cloned.1.call-done = f32[2048,65]{0,1:T(8,128)} async-done(((f32[2048,65]{0,1:T(8,128)}), f32[2048,65]{0,1:T(8,128)}) %all-reduce.3.cloned.1.call-update) | async-done | bytes 532496 | tf_op jit(solution)/shard_map/psum | solution.py:91
  478.4 381.5 %while.31 = (s32[]{:T(128)}, f32[16384,65]{0,1:T(8,128)}, s32[2048]{0:T(1024)}, s32[]{:T(128)}, bf16[2048,65]{0,1:T(8,128)(2,1)S(1)}, /*index=5*/s32[]{:T(128)}, s32[]{:T(128)}, s32[]{:T(128)}, s32[]{:T(128)}) while((s32[]{:T(128)}, f32[16384,65]{0,1:T(8,128)}, s32[2048]{0:T(1024)}, s32[]{:T(128)}, bf16[2048,65]{0,1:T(8,128)(2,1)S(1)}, ...), condition=%wide.region_4.5_spmd.clone, body=%wide.region_3.4_spmd.clone.sunk | while | flops 1461882368 | bytes 8730785 | solution.py:52
  479.6 93.6 %convolution_add_fusion.2 = f32[16384,65]{0,1:T(8,128)} fusion(s32[16384]{0:T(1024)S(1)} %add_select_fusion.20, s32[512]{0:T(512)S(1)} %add_select_fusion.21, f32[16384,65]{0,1:T(8,128)} %get-tuple-element.400, pred[]{:T(512)S(6)} %compare.19, bf16[2048,65]{0,1:T(8,128)(2,1)S(1)} %get-tuple-element.412, s32[]{:T(128)S(6)} %select_n.397), kind=kOutput, calls=%fused_computation.70.clone.3 | convolution fusion | flops 1461747712 | bytes 8660997 | tf_op jit(solution)/shard_map/while/body/eval_jaxpr/dot_general | solution.py:48
  574.0 94.8 %convolution_add_fusion.2 = f32[16384,65]{0,1:T(8,128)} fusion(s32[16384]{0:T(1024)S(1)} %add_select_fusion.20, s32[512]{0:T(512)S(1)} %add_select_fusion.21, f32[16384,65]{0,1:T(8,128)} %get-tuple-element.400, pred[]{:T(512)S(6)} %compare.19, bf16[2048,65]{0,1:T(8,128)(2,1)S(1)} %get-tuple-element.412, s32[]{:T(128)S(6)} %select_n.397), kind=kOutput, calls=%fused_computation.70.clone.3 | convolution fusion | flops 1461747712 | bytes 8660997 | tf_op jit(solution)/shard_map/while/body/eval_jaxpr/dot_general | solution.py:48
  669.6 94.8 %convolution_add_fusion.2 = f32[16384,65]{0,1:T(8,128)} fusion(s32[16384]{0:T(1024)S(1)} %add_select_fusion.20, s32[512]{0:T(512)S(1)} %add_select_fusion.21, f32[16384,65]{0,1:T(8,128)} %get-tuple-element.400, pred[]{:T(512)S(6)} %compare.19, bf16[2048,65]{0,1:T(8,128)(2,1)S(1)} %get-tuple-element.412, s32[]{:T(128)S(6)} %select_n.397), kind=kOutput, calls=%fused_computation.70.clone.3 | convolution fusion | flops 1461747712 | bytes 8660997 | tf_op jit(solution)/shard_map/while/body/eval_jaxpr/dot_general | solution.py:48
  765.2 94.8 %convolution_add_fusion.2 = f32[16384,65]{0,1:T(8,128)} fusion(s32[16384]{0:T(1024)S(1)} %add_select_fusion.20, s32[512]{0:T(512)S(1)} %add_select_fusion.21, f32[16384,65]{0,1:T(8,128)} %get-tuple-element.400, pred[]{:T(512)S(6)} %compare.19, bf16[2048,65]{0,1:T(8,128)(2,1)S(1)} %get-tuple-element.412, s32[]{:T(128)S(6)} %select_n.397), kind=kOutput, calls=%fused_computation.70.clone.3 | convolution fusion | flops 1461747712 | bytes 8660997 | tf_op jit(solution)/shard_map/while/body/eval_jaxpr/dot_general | solution.py:48
  860.0 85.3 %reduce-scatter.2.cloned.1.call-done = f32[4096,65]{0,1:T(8,128)} async-done(((f32[16384,65]{0,1:T(8,128)}), f32[4096,65]{0,1:T(8,128)}) %reduce-scatter.2.cloned.1.call-update) | async-done | bytes 1064976 | tf_op jit(solution)/shard_map/reduce_scatter | solution.py:94
  956.0 64.8 %all-reduce = (f32[64,64]{0,1:T(8,128)S(1)}, f32[64,64]{0,1:T(8,128)S(1)}, f32[64]{0:T(128)S(1)}) all-reduce(f32[64,64]{0,1:T(8,128)S(1)} %fusion.91, f32[64,64]{0,1:T(8,128)S(1)} %fusion.78, f32[64]{0:T(128)S(1)} %convolution_bitcast_fusion), channel_id=1, replica_groups=mesh['group'=2,'rows'=4,'sec'=2,'sub'=2] {'rows','sec','sub'}, use_global_device_ids=true, to_apply=%region_7.8 | all-reduce | flops 8256 | bytes 66048 | tf_op jit(solution)/shard_map/psum | solution.py:102
  1021.0 5.8 cholesky.16
  1028.2 4.9 custom-call.8
  1035.3 13.1 %all_gather.6 = f32[16384]{0:T(1024)S(1)} all-gather(f32[4096]{0:T(1024)S(1)} %subtract_multiply_fusion), channel_id=1, replica_groups=mesh['group'=2,'rows'=4,'sec'=2,'sub'=2] {'rows'}, dimensions={0}, use_global_device_ids=true | all-gather | bytes 81920 | tf_op jit(solution)/shard_map/all_gather | solution.py:105
  1049.1 4.5 copy.62
  (77 shorter events, 36.7 us)
Async XLA Ops:
  7.2 469.1 %all-reduce.3.cloned.1.call-start = ((), (), s32[]{:S(2)}) async-start(), calls=%async_computation.1 | async-start | bytes 1179648 | tf_op jit(solution)/shard_map/psum | solution.py:91
  23.3 453.9 %copy-start.2 = (s32[2048]{0:T(1024)S(1)}, s32[2048]{0:T(1024)}, u32[]{:S(2)}) copy-start(s32[2048]{0:T(1024)} %param.9) | copy-start | bytes 24580
  23.3 91.7 %copy-start = (bf16[16384,65]{1,0:T(8,128)(2,1)S(1)}, bf16[16384,65]{1,0:T(8,128)(2,1)}, u32[]{:S(2)}) copy-start(bf16[16384,65]{1,0:T(8,128)(2,1)} %get-tuple-element.387) | copy-start | bytes 6389764 | tf_op jit(solution)/shard_map/while
  127.2 91.8 %copy-start = (bf16[16384,65]{1,0:T(8,128)(2,1)S(1)}, bf16[16384,65]{1,0:T(8,128)(2,1)}, u32[]{:S(2)}) copy-start(bf16[16384,65]{1,0:T(8,128)(2,1)} %get-tuple-element.387) | copy-start | bytes 6389764 | tf_op jit(solution)/shard_map/while
  231.0 91.8 %copy-start = (bf16[16384,65]{1,0:T(8,128)(2,1)S(1)}, bf16[16384,65]{1,0:T(8,128)(2,1)}, u32[]{:S(2)}) copy-start(bf16[16384,65]{1,0:T(8,128)(2,1)} %get-tuple-element.387) | copy-start | bytes 6389764 | tf_op jit(solution)/shard_map/while
  334.9 91.8 %copy-start = (bf16[16384,65]{1,0:T(8,128)(2,1)S(1)}, bf16[16384,65]{1,0:T(8,128)(2,1)}, u32[]{:S(2)}) copy-start(bf16[16384,65]{1,0:T(8,128)(2,1)} %get-tuple-element.387) | copy-start | bytes 6389764 | tf_op jit(solution)/shard_map/while
  440.0 505.4 %reduce-scatter.2.cloned.1.call-start = ((), (), s32[]{:S(2)}) async-start(), calls=%async_computation.2 | async-start | bytes 5898240 | tf_op jit(solution)/shard_map/reduce_scatter | solution.py:94
  478.4 466.9 %copy-start.1 = (bf16[16384,64]{0,1:T(8,128)(2,1)S(1)}, bf16[16384,64]{0,1:T(8,128)(2,1)}, u32[]{:S(2)}) copy-start(bf16[16384,64]{0,1:T(8,128)(2,1)} %param.11) | copy-start | bytes 6291460
  860.0 188.5 %all-gather.2.cloned.1.call-start = ((), (), s32[]{:S(2)}) async-start(), calls=%async_computation.3 | async-start | bytes 5242880 | tf_op jit(solution)/shard_map/all_gather | solution.py:106
Sparse Core Ops, SparseCore 0:
  440.1 36.1 all-reduce.2
  860.1 85.2 reduce-scatter.1
  947.9 82.4 all-gather.1
where the time goes:
time: 1060 us
  matrix products  422 us (40%)
  other arithmetic  394 us (37%)
  waiting for transfers between devices  122 us (12%)
  blocking collectives  77.9 us (7%)
  local copies, waits for them, and re-layouts  29.7 us (3%)
  between operations  13.9 us (1%)
    dot_general x4, matrix products, add_block(): lax.dot_general(tab, block_mixed, (((0,), (0,)), ((), ())), preferred_ele...  378 us
    dot_general x4, other arithmetic, one_block(): jnp.dot(table_block(block_seeds, first, nfeat), stacked, preferred_elemen...  367 us
    reduce_scatter x1, waiting for transfers between devices, local(): lax.psum_scatter(partial_total, 'rows', scatter_dimension=0, tiled=True)  85.3 us
    psum x1, blocking collectives, local(): core, square, proj = lax.psum((core, square, proj), ('rows', 'sec', 'sub'))  64.8 us
    psum x1, waiting for transfers between devices, local(): margins = lax.psum(local_margins, ('sec', 'sub'))  36.3 us
    dot_general x4, matrix products, one_block(): jnp.dot(table_block(block_seeds, first, nfeat), stacked, preferred_elemen...  35.3 us
  transfers between devices with their start and end apart: 3, of which 2 were waited for; matrix products, arithmetic and copies ran while one was open for 2% of the time, Pallas kernels for 0%

commit v1 on v0

--- a/solution.py
+++ b/solution.py
@@ -88,7 +88,7 @@
     first = lax.axis_index(("sec", "sub")) * nfeat
     stacked = jnp.concatenate([weights.astype(jnp.bfloat16)[:, None], sketch], axis=1)
     local_margins = margin_rows(row_seeds, first, stacked)
-    margins = lax.psum(local_margins, ("sec", "sub"))
+    margins = lax.psum(lax.psum(local_margins, "sub"), "sec")
     mixed = weigh(margins, labels)
     partial_total = accumulate(row_seeds, mixed, first, nfeat)
     piece = lax.psum_scatter(partial_total, "rows", scatter_dimension=0, tiled=True)

time: 1060 us -> 1080 us (1.019)
  waiting for transfers between devices: 122 us -> 141 us
    psum x1 -> x2, waiting for transfers between devices: 36.3 us -> 55.2 us  [local(): margins = lax.psum(lax.psum(local_margins, 'sub'), 'sec')]
  transfers between devices with their start and end apart: 3 -> 4, of which waited for: 2 -> 3; matrix products, arithmetic and copies ran while one was open for 2% -> 2% of each run, Pallas kernels for 0% -> 0%
where the time goes in v1:
time: 1080 us
  matrix products  422 us (39%)
  other arithmetic  394 us (36%)
  waiting for transfers between devices  141 us (13%)
  blocking collectives  78 us (7%)
  local copies, waits for them, and re-layouts  29.7 us (3%)
  between operations  13.9 us (1%)
    dot_general x4, matrix products, add_block(): lax.dot_general(tab, block_mixed, (((0,), (0,)), ((), ())), preferred_ele...  378 us
    dot_general x4, other arithmetic, one_block(): jnp.dot(table_block(block_seeds, first, nfeat), stacked, preferred_elemen...  367 us
    reduce_scatter x1, waiting for transfers between devices, local(): lax.psum_scatter(partial_total, 'rows', scatter_dimension=0, tiled=True)  85.4 us
    psum x1, blocking collectives, local(): core, square, proj = lax.psum((core, square, proj), ('rows', 'sec', 'sub'))  64.8 us
    psum x2, waiting for transfers between devices, local(): margins = lax.psum(lax.psum(local_margins, 'sub'), 'sec')  55.2 us
    dot_general x4, matrix products, one_block(): jnp.dot(table_block(block_seeds, first, nfeat), stacked, preferred_elemen...  35.3 us
  transfers between devices with their start and end apart: 4, of which 3 were waited for; matrix products, arithmetic and copies ran while one was open for 2% of the time, Pallas kernels for 0%

profile of v1, /device:TPU:0, one launch (start us, length us, event | category | flops | bytes accessed | tf_op | source)
XLA Modules:
  0.0 1079.3 jit_solution(16345287337990603157)
XLA Ops:
  11.9 4.7 copy.29
  17.4 5.9 pad_maximum_fusion
  23.3 415.5 %while.30 = (s32[]{:T(128)}, f32[4,512,65]{1,0,2:T(4,128)S(1)}, s32[4,512]{1,0:T(4,128)S(1)}, s32[]{:T(128)}, bf16[16384,65]{1,0:T(8,128)(2,1)}, /*index=5*/s32[]{:T(128)}, s32[]{:T(128)}) while((s32[]{:T(128)}, f32[4,512,65]{1,0,2:T(4,128)S(1)}, s32[4,512]{1,0:T(4,128)S(1)}, s32[]{:T(128)}, bf16[16384,65]{1,0:T(8,128)(2,1)}, ...), condition=%wide.region_1.2_spmd, body=%wide.region_0.1_spmd.sunk | while | flops 1459752448 | bytes 45011060 | solution.py:36
  23.4 91.7 %fusion.121 = bf16[512,16384]{1,0:T(8,128)(2,1)} fusion(s32[16384]{0:T(1024)S(1)} %add_select_fusion.18, s32[512]{0:T(512)S(1)} %add_select_fusion.19), kind=kLoop, calls=%fused_computation.18.clone.clone.clone.clone.1.clone.1 | loop fusion | flops 369098752 | bytes 16844800 | tf_op jit(solution)/shard_map/while/body/eval_jaxpr/dot_general | solution.py:32
  115.0 8.8 fusion.122
  127.3 91.7 %fusion.121 = bf16[512,16384]{1,0:T(8,128)(2,1)} fusion(s32[16384]{0:T(1024)S(1)} %add_select_fusion.18, s32[512]{0:T(512)S(1)} %add_select_fusion.19), kind=kLoop, calls=%fused_computation.18.clone.clone.clone.clone.1.clone.1 | loop fusion | flops 369098752 | bytes 16844800 | tf_op jit(solution)/shard_map/while/body/eval_jaxpr/dot_general | solution.py:32
  218.9 8.8 fusion.122
  231.1 91.7 %fusion.121 = bf16[512,16384]{1,0:T(8,128)(2,1)} fusion(s32[16384]{0:T(1024)S(1)} %add_select_fusion.18, s32[512]{0:T(512)S(1)} %add_select_fusion.19), kind=kLoop, calls=%fused_computation.18.clone.clone.clone.clone.1.clone.1 | loop fusion | flops 369098752 | bytes 16844800 | tf_op jit(solution)/shard_map/while/body/eval_jaxpr/dot_general | solution.py:32
  322.8 8.8 fusion.122
  335.0 91.7 %fusion.121 = bf16[512,16384]{1,0:T(8,128)(2,1)} fusion(s32[16384]{0:T(1024)S(1)} %add_select_fusion.18, s32[512]{0:T(512)S(1)} %add_select_fusion.19), kind=kLoop, calls=%fused_computation.18.clone.clone.clone.clone.1.clone.1 | loop fusion | flops 369098752 | bytes 16844800 | tf_op jit(solution)/shard_map/while/body/eval_jaxpr/dot_general | solution.py:32
  426.7 8.8 fusion.122
  440.0 21.6 %all-reduce.4.cloned.1.call-done = f32[2048,65]{0,1:T(8,128)} async-done(((f32[2048,65]{0,1:T(8,128)}), f32[2048,65]{0,1:T(8,128)}) %all-reduce.4.cloned.1.call-update) | async-done | bytes 532496 | tf_op jit(solution)/shard_map/psum | solution.py:91
  461.7 33.6 %all-reduce.6.cloned.1.call-done = f32[2048,65]{0,1:T(8,128)} async-done(((f32[2048,65]{0,1:T(8,128)}), f32[2048,65]{0,1:T(8,128)}) %all-reduce.6.cloned.1.call-update) | async-done | bytes 532496 | tf_op jit(solution)/shard_map/psum | solution.py:91
  497.4 381.5 %while.31 = (s32[]{:T(128)}, f32[16384,65]{0,1:T(8,128)}, s32[2048]{0:T(1024)}, s32[]{:T(128)}, bf16[2048,65]{0,1:T(8,128)(2,1)S(1)}, /*index=5*/s32[]{:T(128)}, s32[]{:T(128)}, s32[]{:T(128)}, s32[]{:T(128)}) while((s32[]{:T(128)}, f32[16384,65]{0,1:T(8,128)}, s32[2048]{0:T(1024)}, s32[]{:T(128)}, bf16[2048,65]{0,1:T(8,128)(2,1)S(1)}, ...), condition=%wide.region_5.6_spmd.clone, body=%wide.region_4.5_spmd.clone.sunk | while | flops 1461882368 | bytes 8730785 | solution.py:52
  498.6 93.6 %convolution_add_fusion.2 = f32[16384,65]{0,1:T(8,128)} fusion(s32[16384]{0:T(1024)S(1)} %add_select_fusion.20, s32[512]{0:T(512)S(1)} %add_select_fusion.21, f32[16384,65]{0,1:T(8,128)} %get-tuple-element.400, pred[]{:T(512)S(6)} %compare.19, bf16[2048,65]{0,1:T(8,128)(2,1)S(1)} %get-tuple-element.412, s32[]{:T(128)S(6)} %select_n.397), kind=kOutput, calls=%fused_computation.70.clone.3 | convolution fusion | flops 1461747712 | bytes 8660997 | tf_op jit(solution)/shard_map/while/body/eval_jaxpr/dot_general | solution.py:48
  593.0 94.8 %convolution_add_fusion.2 = f32[16384,65]{0,1:T(8,128)} fusion(s32[16384]{0:T(1024)S(1)} %add_select_fusion.20, s32[512]{0:T(512)S(1)} %add_select_fusion.21, f32[16384,65]{0,1:T(8,128)} %get-tuple-element.400, pred[]{:T(512)S(6)} %compare.19, bf16[2048,65]{0,1:T(8,128)(2,1)S(1)} %get-tuple-element.412, s32[]{:T(128)S(6)} %select_n.397), kind=kOutput, calls=%fused_computation.70.clone.3 | convolution fusion | flops 1461747712 | bytes 8660997 | tf_op jit(solution)/shard_map/while/body/eval_jaxpr/dot_general | solution.py:48
  688.6 94.8 %convolution_add_fusion.2 = f32[16384,65]{0,1:T(8,128)} fusion(s32[16384]{0:T(1024)S(1)} %add_select_fusion.20, s32[512]{0:T(512)S(1)} %add_select_fusion.21, f32[16384,65]{0,1:T(8,128)} %get-tuple-element.400, pred[]{:T(512)S(6)} %compare.19, bf16[2048,65]{0,1:T(8,128)(2,1)S(1)} %get-tuple-element.412, s32[]{:T(128)S(6)} %select_n.397), kind=kOutput, calls=%fused_computation.70.clone.3 | convolution fusion | flops 1461747712 | bytes 8660997 | tf_op jit(solution)/shard_map/while/body/eval_jaxpr/dot_general | solution.py:48
  784.2 94.8 %convolution_add_fusion.2 = f32[16384,65]{0,1:T(8,128)} fusion(s32[16384]{0:T(1024)S(1)} %add_select_fusion.20, s32[512]{0:T(512)S(1)} %add_select_fusion.21, f32[16384,65]{0,1:T(8,128)} %get-tuple-element.400, pred[]{:T(512)S(6)} %compare.19, bf16[2048,65]{0,1:T(8,128)(2,1)S(1)} %get-tuple-element.412, s32[]{:T(128)S(6)} %select_n.397), kind=kOutput, calls=%fused_computation.70.clone.3 | convolution fusion | flops 1461747712 | bytes 8660997 | tf_op jit(solution)/shard_map/while/body/eval_jaxpr/dot_general | solution.py:48
  879.0 85.4 %reduce-scatter.2.cloned.1.call-done = f32[4096,65]{0,1:T(8,128)} async-done(((f32[16384,65]{0,1:T(8,128)}), f32[4096,65]{0,1:T(8,128)}) %reduce-scatter.2.cloned.1.call-update) | async-done | bytes 1064976 | tf_op jit(solution)/shard_map/reduce_scatter | solution.py:94
  975.1 64.8 %all-reduce = (f32[64,64]{0,1:T(8,128)S(1)}, f32[64,64]{0,1:T(8,128)S(1)}, f32[64]{0:T(128)S(1)}) all-reduce(f32[64,64]{0,1:T(8,128)S(1)} %fusion.91, f32[64,64]{0,1:T(8,128)S(1)} %fusion.78, f32[64]{0:T(128)S(1)} %convolution_bitcast_fusion), channel_id=1, replica_groups=mesh['group'=2,'rows'=4,'sec'=2,'sub'=2] {'rows','sec','sub'}, use_global_device_ids=true, to_apply=%region_8.9 | all-reduce | flops 8256 | bytes 66048 | tf_op jit(solution)/shard_map/psum | solution.py:102
  1040.1 5.8 cholesky.16
  1047.2 4.9 custom-call.8
  1054.4 13.2 %all_gather.6 = f32[16384]{0:T(1024)S(1)} all-gather(f32[4096]{0:T(1024)S(1)} %subtract_multiply_fusion), channel_id=1, replica_groups=mesh['group'=2,'rows'=4,'sec'=2,'sub'=2] {'rows'}, dimensions={0}, use_global_device_ids=true | all-gather | bytes 81920 | tf_op jit(solution)/shard_map/all_gather | solution.py:105
  1068.2 4.5 copy.63
  (80 shorter events, 40.5 us)
Async XLA Ops:
  7.2 454.5 %all-reduce.4.cloned.1.call-start = ((), (), s32[]{:S(2)}) async-start(), calls=%async_computation.1 | async-start | bytes 1179648 | tf_op jit(solution)/shard_map/psum | solution.py:91
  23.3 472.9 %copy-start.2 = (s32[2048]{0:T(1024)S(1)}, s32[2048]{0:T(1024)}, u32[]{:S(2)}) copy-start(s32[2048]{0:T(1024)} %param.9) | copy-start | bytes 24580
  23.3 91.7 %copy-start = (bf16[16384,65]{1,0:T(8,128)(2,1)S(1)}, bf16[16384,65]{1,0:T(8,128)(2,1)}, u32[]{:S(2)}) copy-start(bf16[16384,65]{1,0:T(8,128)(2,1)} %get-tuple-element.387) | copy-start | bytes 6389764 | tf_op jit(solution)/shard_map/while
  127.2 91.8 %copy-start = (bf16[16384,65]{1,0:T(8,128)(2,1)S(1)}, bf16[16384,65]{1,0:T(8,128)(2,1)}, u32[]{:S(2)}) copy-start(bf16[16384,65]{1,0:T(8,128)(2,1)} %get-tuple-element.387) | copy-start | bytes 6389764 | tf_op jit(solution)/shard_map/while
  231.0 91.8 %copy-start = (bf16[16384,65]{1,0:T(8,128)(2,1)S(1)}, bf16[16384,65]{1,0:T(8,128)(2,1)}, u32[]{:S(2)}) copy-start(bf16[16384,65]{1,0:T(8,128)(2,1)} %get-tuple-element.387) | copy-start | bytes 6389764 | tf_op jit(solution)/shard_map/while
  334.9 91.8 %copy-start = (bf16[16384,65]{1,0:T(8,128)(2,1)S(1)}, bf16[16384,65]{1,0:T(8,128)(2,1)}, u32[]{:S(2)}) copy-start(bf16[16384,65]{1,0:T(8,128)(2,1)} %get-tuple-element.387) | copy-start | bytes 6389764 | tf_op jit(solution)/shard_map/while
  440.0 55.4 %all-reduce.6.cloned.1.call-start = ((), (), s32[]{:S(2)}) async-start(), calls=%async_computation.2 | async-start | bytes 1179648 | tf_op jit(solution)/shard_map/psum | solution.py:91
  461.7 502.7 %reduce-scatter.2.cloned.1.call-start = ((), (), s32[]{:S(2)}) async-start(), calls=%async_computation.3 | async-start | bytes 5898240 | tf_op jit(solution)/shard_map/reduce_scatter | solution.py:94
  497.4 467.0 %copy-start.1 = (bf16[16384,64]{0,1:T(8,128)(2,1)S(1)}, bf16[16384,64]{0,1:T(8,128)(2,1)}, u32[]{:S(2)}) copy-start(bf16[16384,64]{0,1:T(8,128)(2,1)} %param.11) | copy-start | bytes 6291460
  879.0 188.6 %all-gather.2.cloned.1.call-start = ((), (), s32[]{:S(2)}) async-start(), calls=%async_computation.4 | async-start | bytes 5242880 | tf_op jit(solution)/shard_map/all_gather | solution.py:106
Sparse Core Ops, SparseCore 0:
  440.1 21.5 all-reduce.3
  464.1 31.2 all-reduce.5
  879.1 85.2 reduce-scatter.1
  967.0 82.4 all-gather.1
